TPU v7x, 32 devices: a whole 2x2x4 slice. The times are simulated.
32 devices in a mesh: ep: 8 (over z, x), rep: 4 (over y, core).
Axes of the slice: x: 2, y: 2, z: 4, core: 2. Of those that a mesh axis runs over, the one named last changes fastest.
Arguments:
- context: bfloat16 [2048, 2048], P(('ep', 'rep')), may hold values from -6 to 6
- residual: bfloat16 [2048, 2048], P(('ep', 'rep')), may hold values from -125 to 125
- out_proj: bfloat16 [2048, 2048], replicated, may hold values from -0.125 to 0.125
- attn_gain: bfloat16 [2048], replicated, may hold values from 0.25 to 1.75
- router: bfloat16 [2048, 64], replicated, may hold values from -18 to 18
- expert_ids: int32 [2048, 8], P(('ep', 'rep')), may hold values from 0 to 63, as said below
- gate_weight: bfloat16 [64, 2048, 1024], P('ep', None, 'rep'), may hold values from -0.125 to 0.125
- up_weight: bfloat16 [64, 2048, 1024], P('ep', None, 'rep'), may hold values from -0.125 to 0.125
- down_weight: bfloat16 [64, 2048, 1024], P('ep', None, 'rep'), may hold values from -1.5 to 1.5
- final_gain: bfloat16 [2048], replicated, may hold values from 0.25 to 1.75
Outputs:
- layer_out: bfloat16 [2048, 2048], P(('ep', 'rep'))
Inputs may be any that keep to these rules, and one draw needn't show every extreme that they name: `expert_ids`: the rows of one device name exactly 32 distinct experts, each of them exactly 16 times. The entries of a row are distinct. Every expert is named by some row.
All inputs are finite; a program needn't handle non-finite values.
Results may differ from a plain program's by a relative error of at most 0.005.
Values may be sent and summed in bfloat16 or wider, within the bound.
A program may use at most 192 MiB of HBM per device.

v0:
```python
import jax
import jax.numpy as jnp
from jax import lax
from jax.sharding import PartitionSpec as P

epsilon = 1e-05


def rms_scale(values, gain_vector):
    mean_square = jnp.mean(values * values, axis=-1, keepdims=True)
    return values * lax.rsqrt(mean_square + epsilon) * gain_vector.astype(jnp.float32)


def expert_part(batch_rows, gate_piece, up_piece, down_piece):
    gate_proj = jnp.einsum(
        "xnd,xdw->xnw", batch_rows, gate_piece, preferred_element_type=jnp.float32
    )
    up_proj = jnp.einsum("xnd,xdw->xnw", batch_rows, up_piece, preferred_element_type=jnp.float32)
    active = (jax.nn.silu(gate_proj) * up_proj).astype(jnp.bfloat16)
    part_sum = jnp.einsum("xnw,xdw->xnd", active, down_piece, preferred_element_type=jnp.float32)
    return lax.optimization_barrier(part_sum.astype(jnp.bfloat16)).astype(jnp.float32)


def per_device(
    context,
    residual,
    out_proj,
    attn_gain,
    router,
    expert_ids,
    gate_weight,
    up_weight,
    down_weight,
    final_gain,
):
    row_count, model_width = context.shape
    top_count = expert_ids.shape[1]
    expert_count = router.shape[1]
    owners = lax.axis_size("ep")
    local_experts = gate_weight.shape[0]
    slot_count = row_count // 4
    attention = jnp.dot(context, out_proj, preferred_element_type=jnp.float32)
    mixed_stream = residual.astype(jnp.float32) + attention
    normed = rms_scale(mixed_stream, attn_gain).astype(jnp.bfloat16)
    logits = jnp.dot(normed, router, preferred_element_type=jnp.float32)
    probs = jax.nn.softmax(logits, axis=1)
    route_weight = jnp.take_along_axis(probs, expert_ids, axis=1)
    flat_ids = expert_ids.reshape(-1)
    one_hot = (flat_ids[:, None] == jnp.arange(expert_count, dtype=jnp.int32)[None, :]).astype(
        jnp.int32
    )
    slot_rank = jnp.sum(jnp.cumsum(one_hot, axis=0) * one_hot, axis=1) - 1
    slot_index = flat_ids * slot_count + slot_rank
    placing = (
        slot_index[:, None] == jnp.arange(expert_count * slot_count, dtype=jnp.int32)[None, :]
    ).astype(jnp.bfloat16)
    placing = jnp.sum(placing.reshape(row_count, top_count, expert_count * slot_count), axis=1)
    outbound = jnp.einsum("rs,rd->sd", placing, normed, preferred_element_type=jnp.float32).astype(
        jnp.bfloat16
    )
    outbound = outbound.reshape(owners, local_experts * slot_count, model_width)
    received = lax.all_to_all(outbound, "ep", split_axis=0, concat_axis=0, tiled=True)
    grouped = received.reshape(owners, local_experts, slot_count, model_width).transpose(1, 0, 2, 3)
    grouped = grouped.reshape(local_experts, owners * slot_count, model_width)
    partial_terms = expert_part(
        lax.all_gather(grouped, "rep", axis=1, tiled=True), gate_weight, up_weight, down_weight
    )
    expert_out = lax.psum_scatter(
        partial_terms.astype(jnp.bfloat16), "rep", scatter_dimension=1, tiled=True
    )
    outgoing = expert_out.reshape(local_experts, owners, slot_count, model_width).transpose(
        1, 0, 2, 3
    )
    outgoing = outgoing.reshape(owners, local_experts * slot_count, model_width)
    returned = lax.all_to_all(outgoing, "ep", split_axis=0, concat_axis=0, tiled=True)
    returned = returned.reshape(expert_count * slot_count, model_width)
    picked = jnp.take(returned, slot_index, axis=0).reshape(row_count, top_count, model_width)
    expert_mix = jnp.einsum("rk,rkd->rd", route_weight, picked.astype(jnp.float32))
    total = mixed_stream + expert_mix
    return rms_scale(total, final_gain).astype(jnp.bfloat16)


def solution(mesh):
    in_specs = (
        P(("ep", "rep"), None),
        P(("ep", "rep"), None),
        P(),
        P(),
        P(),
        P(("ep", "rep"), None),
        P("ep", None, "rep"),
        P("ep", None, "rep"),
        P("ep", None, "rep"),
        P(),
    )
    out_specs = P(("ep", "rep"), None)
    return jax.shard_map(
        per_device, mesh=mesh, in_specs=in_specs, out_specs=out_specs, check_vma=False
    )
```

profile of v0, /device:TPU:0, one launch (start us, length us, event | category | flops | bytes accessed | tf_op | source)
XLA Modules:
  0.0 513.0 jit_solution(1726489421886921083)
XLA Ops:
  6.5 0.0 copy-start
  6.5 0.0 all-gather.2.cloned.1.call-start
  6.5 0.8 copy.38
  7.4 0.1 eq.40
  7.4 0.1 reshape.131
  7.6 1.2 reduce-window.6
  8.8 0.2 slice_reduce_fusion
  9.0 0.1 fusion.9
  9.2 0.1 sub.19
  9.3 0.1 copy.41
  9.3 0.7 compare_and_fusion
  10.0 0.1 copy.43
  10.1 0.7 fusion.6
  10.8 0.0 copy-done
  10.8 0.0 copy-start.4
  10.8 5.1 multiply_reduce_fusion.1
  15.9 0.0 copy-done.4
  15.9 1.3 convolution_convert_fusion.1
  17.3 100.2 %all_to_all.10 = bf16[8,128,2048]{2,1,0:T(8,128)(2,1)S(1)} all-to-all(bf16[8,128,2048]{2,1,0:T(8,128)(2,1)S(1)} %bitcast.54), channel_id=1, replica_groups=mesh['ep'=8,'rep'=4] {'ep'}, dimensions={0} | all-to-all | bytes 8388608 | tf_op jit(solution)/shard_map/all_to_all | solution.py:62
  117.5 2.2 copy.44
  119.7 0.0 all-gather.2.cloned.1.call-update
  119.8 0.2 reduce-scatter.2.cloned.1.call-start
  120.0 104.9 %all-gather.2.cloned.1.call-done = bf16[8,512,2048]{2,1,0:T(8,128)(2,1)} async-done(((bf16[8,128,2048]{2,1,0:T(8,128)(2,1)}), bf16[8,512,2048]{2,1,0:T(8,128)(2,1)}) %all-gather.2.cloned.1.call-update) | async-done | bytes 16777232 | tf_op jit(solution)/shard_map/all_gather | solution.py:66
  224.9 14.7 %fusion.19 = f32[8,512,256]{2,1,0:T(8,128)} fusion(bf16[8,512,2048]{2,1,0:T(8,128)(2,1)} %all-gather.2.cloned.1.call-done, bf16[8,2048,256]{2,1,0:T(8,128)(2,1)} %param.16), kind=kOutput, calls=%fused_computation.47 | convolution fusion | flops 4294967296 | bytes 29360128 | tf_op jit(solution)/shard_map/xnd,xdw->xnw/dot_general | solution.py:15
  239.6 27.5 %convolution_convert_fusion = bf16[8,512,2048]{2,1,0:T(8,128)(2,1)} fusion(bf16[8,2048,256]{2,1,0:T(8,128)(2,1)} %param.18, f32[8,512,256]{2,1,0:T(8,128)} %fusion.19, bf16[8,512,2048]{2,1,0:T(8,128)(2,1)} %all-gather.2.cloned.1.call-done, bf16[8,2048,256]{2,1,0:T(8,128)(2,1)} %param.17), kind=kOutput, calls=%fused_computation.2 | convolution fusion | flops 8604614656 | bytes 54525952 | tf_op jit(solution)/shard_map/xnw,xdw->xnd/dot_general | solution.py:20
  267.0 0.0 reduce-scatter.2.cloned.1.call-update
  267.1 126.3 %reduce-scatter.2.cloned.1.call-done = bf16[8,128,2048]{2,1,0:T(8,128)(2,1)} async-done(((bf16[8,512,2048]{2,1,0:T(8,128)(2,1)}), bf16[8,128,2048]{2,1,0:T(8,128)(2,1)}) %reduce-scatter.2.cloned.1.call-update) | async-done | bytes 4194320 | tf_op jit(solution)/shard_map/reduce_scatter | solution.py:68
  393.3 4.7 copy.45
  398.1 0.0 copy-start.3
  398.1 0.0 copy-start.2
  398.1 5.6 %all-to-all-start.1 = ((bf16[8,128,2048]{2,1,0:T(8,128)(2,1)}), bf16[8,128,2048]{2,1,0:T(8,128)(2,1)}, u32[]{:S(2)}, u32[]{:S(2)}) async-start(bf16[8,128,2048]{2,1,0:T(8,128)(2,1)} %bitcast.52), calls=%async_computation.2 | async-start | bytes 8388608 | tf_op jit(solution)/shard_map/all_to_all | solution.py:75
  403.7 0.0 copy-done.3
  403.7 0.1 copy.46
  403.8 0.1 mul.80
  403.9 0.1 copy.36
  404.0 0.1 reshape.147
  404.1 0.0 copy-done.2
  404.1 0.3 fusion.18
  404.5 0.0 copy-start.5
  404.5 4.7 gather_fusion.1
  409.2 0.1 reshape.150
  409.3 0.1 copy.37
  409.4 0.1 copy.47
  409.5 0.1 copy.42
  409.6 0.0 copy-done.5
  409.7 87.3 %all-to-all-done.1 = bf16[8,128,2048]{2,1,0:T(8,128)(2,1)} async-done(((bf16[8,128,2048]{2,1,0:T(8,128)(2,1)}), bf16[8,128,2048]{2,1,0:T(8,128)(2,1)}, u32[]{:S(2)}, u32[]{:S(2)}) %all-to-all-start.1) | async-done | bytes 4194336 | tf_op jit(solution)/shard_map/all_to_all | solution.py:75
  497.0 0.0 copy-start.1
  497.0 7.2 %gather_fusion = bf16[512,2048]{1,0:T(8,128)(2,1)S(1)} fusion(bf16[1024,2048]{1,0:T(8,128)(2,1)} %bitcast.10, s32[1024]{0:T(1024)S(1)} %pad_clamp_fusion), kind=kCustom, calls=%fused_computation | custom fusion | bytes 4196352 | tf_op jit(solution)/shard_map/jit(_take)/gather | solution.py:77
  504.2 0.8 fusion.2
  505.0 0.3 multiply_reduce_fusion
  505.2 0.9 multiply_convert_fusion.2
  506.1 0.0 copy-done.1
  (15 shorter events, 0.2 us)
Async XLA Ops:
  6.5 4.3 copy-start
  6.5 218.3 %all-gather.2.cloned.1.call-start = ((), (), s32[]{:S(2)}) async-start(), calls=%async_computation.3 | async-start | bytes 20971520 | tf_op jit(solution)/shard_map/all_gather | solution.py:66
  10.8 5.1 copy-start.4
  119.8 273.6 %reduce-scatter.2.cloned.1.call-start = ((), (), s32[]{:S(2)}) async-start(), calls=%async_computation.4 | async-start | bytes 20971520 | tf_op jit(solution)/shard_map/reduce_scatter | solution.py:68
  398.1 5.6 %copy-start.3 = (s32[64,8]{0,1:T(8,128)S(1)}, s32[64,8]{0,1:T(8,128)}, u32[]{:S(2)}) copy-start(s32[64,8]{0,1:T(8,128)} %param.15) | copy-start | bytes 6148
  398.1 6.0 %copy-start.2 = (bf16[2048,64]{0,1:T(8,128)(2,1)S(1)}, bf16[2048,64]{0,1:T(8,128)(2,1)}, u32[]{:S(2)}) copy-start(bf16[2048,64]{0,1:T(8,128)(2,1)} %param.14) | copy-start | bytes 786436
  398.1 98.9 %all-to-all-start.1 = ((bf16[8,128,2048]{2,1,0:T(8,128)(2,1)}), bf16[8,128,2048]{2,1,0:T(8,128)(2,1)}, u32[]{:S(2)}, u32[]{:S(2)}) async-start(bf16[8,128,2048]{2,1,0:T(8,128)(2,1)} %bitcast.52), calls=%async_computation.2 | async-start | bytes 8388608 | tf_op jit(solution)/shard_map/all_to_all | solution.py:75
  404.5 5.1 copy-start.5
  497.0 9.2 %copy-start.1 = (bf16[64,2048]{1,0:T(8,128)(2,1)S(1)}, bf16[64,2048]{1,0:T(8,128)(2,1)}, u32[]{:S(2)}) copy-start(bf16[64,2048]{1,0:T(8,128)(2,1)} %param.10) | copy-start | bytes 786436
Sparse Core Ops, SparseCore 0:
  119.9 104.9 all-gather.1
  267.2 126.1 reduce-scatter.1
where the time goes:
time: 513 us
  waiting for transfers between devices  319 us (62%)
  blocking collectives  100 us (19%)
  matrix products  49.6 us (10%)
  local copies, waits for them, and re-layouts  21.1 us (4%)
  between operations  13.6 us (3%)
  starting transfers between devices  5.87 us (1%)
    reduce_scatter x1, waiting for transfers between devices, per_device(): lax.psum_scatter(partial_terms.astype(jnp.bfloat16), 'rep', scatter_dimen...  126 us
    all_gather x1, waiting for transfers between devices, per_device(): lax.all_gather(grouped, 'rep', axis=1, tiled=True)  105 us
    all_to_all x1, blocking collectives, per_device(): lax.all_to_all(outbound, 'ep', split_axis=0, concat_axis=0, tiled=True)  100 us
    all_to_all x1, waiting for transfers between devices, per_device(): lax.all_to_all(outgoing, 'ep', split_axis=0, concat_axis=0, tiled=True)  87.3 us
    dot_general x1, matrix products, expert_part(): jnp.einsum('xnw,xdw->xnd', active, down_piece, preferred_element_type=jnp...  27.5 us
    dot_general x1, matrix products, expert_part(): jnp.einsum('xnd,xdw->xnw', batch_rows, gate_piece, preferred_element_type...  14.7 us
  transfers between devices with their start and end apart: 3, of which 3 were waited for; matrix products, arithmetic and copies ran while one was open for 1% of the time, Pallas kernels for 0%

commit v1 on v0

v1 whole, which is shorter than its diff:
```python
import jax
import jax.numpy as jnp
from jax import lax
from jax.sharding import PartitionSpec as P

epsilon = 1e-05
capacity = 16


def rms_scale(values, gain_vector):
    mean_square = jnp.mean(values * values, axis=-1, keepdims=True)
    return values * lax.rsqrt(mean_square + epsilon) * gain_vector.astype(jnp.float32)


def front(context, residual, out_proj, attn_gain, router, expert_ids):
    expert_count = router.shape[1]
    attention = jnp.dot(context, out_proj, preferred_element_type=jnp.float32)
    mixed_stream = residual.astype(jnp.float32) + attention
    normed = rms_scale(mixed_stream, attn_gain).astype(jnp.bfloat16)
    logits = jnp.dot(normed, router, preferred_element_type=jnp.float32)
    probs = jax.nn.softmax(logits, axis=1)
    chosen = jnp.any(
        expert_ids[:, :, None] == jnp.arange(expert_count, dtype=jnp.int32)[None, None, :], axis=1
    )
    weights = jnp.where(chosen, probs, 0.0)
    return mixed_stream, normed, weights


def gathered(
    context, residual, out_proj, attn_gain, router, expert_ids,
    gate_weight, up_weight, down_weight, final_gain,
):
    row_count, model_width = context.shape
    local_experts = gate_weight.shape[0]
    owners = lax.axis_size("ep")
    sources = owners * lax.axis_size("rep")
    mixed_stream, normed, weights = front(
        context, residual, out_proj, attn_gain, router, expert_ids
    )
    high = weights.astype(jnp.bfloat16)
    low = (weights - high.astype(jnp.float32)).astype(jnp.bfloat16)
    block = jnp.concatenate([normed, high, low], axis=1)
    everyone = lax.all_gather(block, ("ep", "rep"), axis=0, tiled=False)
    rows = everyone[:, :, :model_width]
    first = model_width + lax.axis_index("ep") * local_experts
    high = lax.dynamic_slice_in_dim(everyone, first, local_experts, axis=2)
    low = lax.dynamic_slice_in_dim(everyone, first + weights.shape[1], local_experts, axis=2)
    local_weights = high.astype(jnp.float32) + low.astype(jnp.float32)
    mask = (local_weights > 0).astype(jnp.float32)
    earlier = (
        jnp.arange(row_count)[:, None] > jnp.arange(row_count)[None, :]
    ).astype(jnp.float32)
    rank = jnp.einsum("ij,sje->sie", earlier, mask)
    slots = jnp.arange(capacity, dtype=jnp.float32)
    placing = jnp.where(
        (rank[:, :, :, None] == slots) & (mask[:, :, :, None] > 0), 1.0, 0.0
    )
    slot_weight = jnp.sum(placing * local_weights[:, :, :, None], axis=1)
    placing = placing.astype(jnp.bfloat16).reshape(sources, row_count, local_experts * capacity)
    grouped = jnp.einsum(
        "sit,sid->std", placing, rows, preferred_element_type=jnp.float32
    ).astype(jnp.bfloat16)
    grouped = grouped.reshape(sources, local_experts, capacity, model_width)
    gate_proj = jnp.einsum(
        "serd,edw->serw", grouped, gate_weight, preferred_element_type=jnp.float32
    )
    up_proj = jnp.einsum("serd,edw->serw", grouped, up_weight, preferred_element_type=jnp.float32)
    active = (jax.nn.silu(gate_proj) * up_proj * slot_weight[..., None]).astype(jnp.bfloat16)
    part = jnp.einsum(
        "serw,edw->serd", active, down_weight, preferred_element_type=jnp.float32
    ).astype(jnp.bfloat16)
    part = part.reshape(sources, local_experts * capacity, model_width)
    share = jnp.einsum("sit,std->sid", placing, part, preferred_element_type=jnp.float32)
    share = share.astype(jnp.bfloat16).reshape(sources * row_count, model_width)
    expert_mix = lax.psum_scatter(share, ("ep", "rep"), scatter_dimension=0, tiled=True)
    total = mixed_stream + expert_mix.astype(jnp.float32)
    return rms_scale(total, final_gain).astype(jnp.bfloat16)


def solution(mesh):
    in_specs = (
        P(("ep", "rep"), None),
        P(("ep", "rep"), None),
        P(),
        P(),
        P(),
        P(("ep", "rep"), None),
        P("ep", None, "rep"),
        P("ep", None, "rep"),
        P("ep", None, "rep"),
        P(),
    )
    out_specs = P(("ep", "rep"), None)
    return jax.shard_map(
        gathered, mesh=mesh, in_specs=in_specs, out_specs=out_specs, check_vma=False
    )
```

time: 513 us -> 330 us (0.64)
  blocking collectives: 100 us -> 0 us
  waiting for transfers between devices: 319 us -> 229 us
  matrix products: 49.6 us -> 59.6 us
  starting transfers between devices: 5.87 us -> 0.08 us
    all_to_all x1 -> x0, blocking collectives: 100 us -> none  [per_device(): lax.all_to_all(outbound, 'ep', split_axis=0, concat_axis=0, tiled=True)]
    all_to_all x1 -> x0, waiting for transfers between devices: 87.3 us -> none  [per_device(): lax.all_to_all(outgoing, 'ep', split_axis=0, concat_axis=0, tiled=True)]
    all_gather x1, waiting for transfers between devices: 105 us -> 82.4 us  [gathered(): everyone = lax.all_gather(block, ('ep', 'rep'), axis=0, tiled=False)]
    reduce_scatter x1, waiting for transfers between devices: 126 us -> 147 us  [gathered(): lax.psum_scatter(share, ('ep', 'rep'), scatter_dimension=0, tiled=True)]
    convert_element_type x0 -> x1, local copies, waits for them, and re-layouts: none -> 14.1 us  [gathered(): part = jnp.einsum('serw,edw->serd', active, down_weight, preferred_elemen...]
    gather x6 -> x0, local copies, waits for them, and re-layouts: 12.2 us -> none  [the longest x1 7.18 us: per_device(): jnp.take(returned, slot_index, axis=0)]
    dot_general x6 -> x7, matrix products: 49.6 us -> 59.6 us  [the longest x1 20.4 us: gathered(): jnp.einsum('serw,edw->serd', active, down_weight, preferred_element_type=...]
    reshape x3 -> x0, local copies, waits for them, and re-layouts: 7.06 us -> none  [the longest x1 4.74 us: per_device(): expert_out.reshape(local_experts, owners, slot_count, model_width)]
  transfers between devices with their start and end apart: 3 -> 2, of which waited for: 3 -> 2; matrix products, arithmetic and copies ran while one was open for 1% -> 0% of each run, Pallas kernels for 0% -> 0%
where the time goes in v1:
time: 330 us
  waiting for transfers between devices  229 us (69%)
  matrix products  59.6 us (18%)
  local copies, waits for them, and re-layouts  23.3 us (7%)
  between operations  13.6 us (4%)
  other arithmetic  4.23 us (1%)
    reduce_scatter x1, waiting for transfers between devices, gathered(): lax.psum_scatter(share, ('ep', 'rep'), scatter_dimension=0, tiled=True)  147 us
    all_gather x1, waiting for transfers between devices, gathered(): everyone = lax.all_gather(block, ('ep', 'rep'), axis=0, tiled=False)  82.4 us
    dot_general x1, matrix products, gathered(): jnp.einsum('serw,edw->serd', active, down_weight, preferred_element_type=...  20.4 us
    convert_element_type x1, local copies, waits for them, and re-layouts, gathered(): part = jnp.einsum('serw,edw->serd', active, down_weight, preferred_elemen...  14.1 us
    dot_general x1, matrix products, gathered(): jnp.einsum('serd,edw->serw', grouped, gate_weight, preferred_element_type...  11.8 us
    dot_general x1, matrix products, gathered(): jnp.einsum('sit,std->sid', placing, part, preferred_element_type=jnp.floa...  11.4 us
    dot_general x1, matrix products, gathered(): jnp.einsum('sit,sid->std', placing, rows, preferred_element_type=jnp.floa...  10.5 us
  transfers between devices with their start and end apart: 2, of which 2 were waited for; matrix products, arithmetic and copies ran while one was open for 0% of the time, Pallas kernels for 0%

profile of v1, /device:TPU:0, one launch (start us, length us, event | category | flops | bytes accessed | tf_op | source)
XLA Modules:
  0.0 330.0 jit_solution(15692546400828916785)
XLA Ops:
  6.5 0.0 copy-start
  6.5 0.0 copy-start.3
  6.5 0.0 copy-start.4
  6.5 0.0 copy-start.2
  6.5 0.0 all-gather.3.cloned.1.call-start
  6.6 0.9 copy-done
  7.5 5.1 %multiply_reduce_fusion.2 = (f32[64]{0:T(128)S(1)}, f32[64,2048]{1,0:T(8,128)S(1)}) fusion(bf16[64,2048]{1,0:T(8,128)(2,1)S(1)} %copy-done, bf16[2048,2048]{1,0:T(8,128)(2,1)} %param.12, bf16[64,2048]{1,0:T(8,128)(2,1)} %param.11), kind=kOutput, calls=%fused_computation.29 | convolution fusion | flops 537395136 | bytes 9437440 | tf_op jit(solution)/shard_map/dot_general | solution.py:17
  12.6 0.0 copy-done.3
  12.6 0.0 copy-done.4
  12.6 0.1 copy.56
  12.7 0.2 fusion.22
  12.9 0.1 multiply_convert_fusion.1
  13.0 0.0 copy-done.2
  13.0 0.3 fusion.29
  13.3 0.2 fusion.26
  13.5 0.1 subtract_convert_fusion
  13.6 0.8 concatenate.3
  14.4 0.0 all-gather.3.cloned.1.call-update
  14.4 0.0 reduce-scatter.2.cloned.1.call-start
  14.5 0.1 eq.43
  14.6 82.4 %all-gather.3.cloned.1.call-done = bf16[2048,2176]{1,0:T(8,128)(2,1)} async-done(((bf16[64,2176]{1,0:T(8,128)(2,1)}), bf16[2048,2176]{1,0:T(8,128)(2,1)}) %all-gather.3.cloned.1.call-update) | async-done | bytes 8912912 | tf_op jit(solution)/shard_map/all_gather | solution.py:43
  96.9 1.6 constant_dynamic-slice_fusion.1
  98.6 0.2 copy.70
  98.8 0.2 copy.71
  99.0 0.1 convert_compare_fusion
  99.1 0.2 convolution_bitcast_fusion
  99.2 0.1 copy.60
  99.3 1.5 eq.40
  100.8 2.2 copy.61
  103.0 0.2 and.14
  103.2 0.6 copy.62
  103.8 0.7 multiply_reduce_fusion
  104.5 10.5 %convolution_convert_fusion = bf16[32,128,2048]{2,1,0:T(8,128)(2,1)} fusion(bf16[32,64,2176]{2,1,0:T(8,128)(2,1)} %bitcast.65, pred[32,64,128]{2,1,0:T(32,128)(4,1)S(1)} %copy.62, f32[32,64,128]{2,1,0:T(8,128)S(1)} %copy.61, f32[128]{0:T(128)S(1)} %eq.43), kind=kOutput, calls=%fused_computation.5 | convolution fusion | flops 1083179008 | bytes 26477056 | tf_op jit(solution)/shard_map/sit,sid->std/dot_general | solution.py:60
  115.0 11.8 %fusion.2 = f32[8,32,16,256]{3,2,1,0:T(8,128)} fusion(bf16[32,8,16,2048]{3,2,1,0:T(8,128)(2,1)} %bitcast.62, bf16[8,2048,256]{2,1,0:T(8,128)(2,1)} %param.16), kind=kOutput, calls=%fused_computation.3 | convolution fusion | flops 4294967296 | bytes 29360128 | tf_op jit(solution)/shard_map/serd,edw->serw/dot_general | solution.py:64
  126.8 20.4 %convert_bitcast_fusion = bf16[32,8,16,2048]{3,2,0,1:T(8,128)(2,1)} fusion(bf16[8,2048,256]{2,1,0:T(8,128)(2,1)} %param.18, f32[8,32,16,256]{3,2,1,0:T(8,128)} %fusion.2, bf16[8,2048,256]{2,1,0:T(8,128)(2,1)} %param.17, bf16[32,8,16,2048]{3,2,1,0:T(8,128)(2,1)} %bitcast.63, f32[32,8,16]{2,0,1:T(8,128)S(1)} %copy.65), kind=kOutput, calls=%fused_computation | convolution fusion | flops 8605663232 | bytes 54542336 | tf_op jit(solution)/shard_map/serw,edw->serd/dot_general | solution.py:69
  147.2 14.1 %copy.66 = bf16[32,8,16,2048]{3,2,1,0:T(8,128)(2,1)} copy(bf16[32,8,16,2048]{3,2,0,1:T(8,128)(2,1)} %convert_bitcast_fusion) | data formatting | bytes 33554432 | tf_op jit(solution)/shard_map/convert_element_type | solution.py:71
  161.3 0.0 copy-start.1
  161.3 11.4 %convolution_convert_fusion.1 = bf16[32,64,2048]{2,1,0:T(8,128)(2,1)} fusion(bf16[32,128,2048]{2,1,0:T(8,128)(2,1)} %bitcast.60, pred[32,64,128]{2,1,0:T(32,128)(4,1)S(1)} %copy.62, f32[32,64,128]{2,1,0:T(8,128)S(1)} %copy.61, f32[128]{0:T(128)S(1)} %eq.43), kind=kOutput, calls=%fused_computation.10 | convolution fusion | flops 1078984704 | bytes 26477056 | tf_op jit(solution)/shard_map/sit,std->sid/dot_general | solution.py:73
  172.7 0.0 copy-start.5
  172.7 0.0 reduce-scatter.2.cloned.1.call-update
  172.7 0.7 copy-done.5
  173.4 146.8 %reduce-scatter.2.cloned.1.call-done = bf16[64,2048]{1,0:T(8,128)(2,1)} async-done(((bf16[2048,2048]{1,0:T(8,128)(2,1)}), bf16[64,2048]{1,0:T(8,128)(2,1)}) %reduce-scatter.2.cloned.1.call-update) | async-done | bytes 262160 | tf_op jit(solution)/shard_map/reduce_scatter | solution.py:75
  320.2 1.1 multiply_reduce_fusion.1
  321.4 1.8 multiply_convert_fusion
  323.1 0.0 copy-done.1
  (7 shorter events, 0.1 us)
Async XLA Ops:
  6.5 1.0 copy-start
  6.5 6.0 %copy-start.3 = (bf16[2048]{0:T(1024)(128)(2,1)S(1)}, bf16[2048]{0:T(1024)(128)(2,1)}, u32[]{:S(2)}) copy-start(bf16[2048]{0:T(1024)(128)(2,1)} %param.13) | copy-start | bytes 12292
  6.5 6.1 %copy-start.4 = (s32[64,8]{0,1:T(8,128)S(1)}, s32[64,8]{0,1:T(8,128)}, u32[]{:S(2)}) copy-start(s32[64,8]{0,1:T(8,128)} %param.15) | copy-start | bytes 6148
  6.5 6.4 %copy-start.2 = (bf16[2048,64]{0,1:T(8,128)(2,1)S(1)}, bf16[2048,64]{0,1:T(8,128)(2,1)}, u32[]{:S(2)}) copy-start(bf16[2048,64]{0,1:T(8,128)(2,1)} %param.14) | copy-start | bytes 786436
  6.5 90.4 %all-gather.3.cloned.1.call-start = ((), (), s32[]{:S(2)}) async-start(), calls=%async_computation.2 | async-start | bytes 9191424 | tf_op jit(solution)/shard_map/all_gather | solution.py:43
  14.4 305.8 %reduce-scatter.2.cloned.1.call-start = ((), (), s32[]{:S(2)}) async-start(), calls=%async_computation.1 | async-start | bytes 8650752 | tf_op jit(solution)/shard_map/reduce_scatter | solution.py:75
  161.3 161.8 %copy-start.1 = (bf16[64,2048]{1,0:T(8,128)(2,1)S(1)}, bf16[64,2048]{1,0:T(8,128)(2,1)}, u32[]{:S(2)}) copy-start(bf16[64,2048]{1,0:T(8,128)(2,1)} %param.10) | copy-start | bytes 786436
  172.7 0.7 copy-start.5
Sparse Core Ops, SparseCore 0:
  14.5 82.3 all-gather.2
  172.8 147.3 reduce-scatter.1

commit v2 on v1

--- a/solution.py
+++ b/solution.py
@@ -1,6 +1,8 @@
 import jax
 import jax.numpy as jnp
 from jax import lax
+from jax.experimental import pallas as pl
+from jax.experimental.pallas import tpu as pltpu
 from jax.sharding import PartitionSpec as P
 
 epsilon = 1e-05
@@ -77,7 +79,300 @@
     return rms_scale(total, final_gain).astype(jnp.bfloat16)
 
 
+MESH = pl.DeviceIdType.MESH
+LINE = 4
+OWN, FLIP_Y, FLIP_X, FLIP_BOTH = 0, 1, 2, 3
+
+
+def box_kernel(
+    block_ref, mixed_ref, gain_ref, gate_hbm, up_hbm, down_hbm, out_ref,
+    rows, gate, up, down, grouped, placing, slot_weight,
+    sibling_share, sibling_sum, share, first_x, first_y, second_x, second_y, column, last,
+    weight_sem, send_sem, recv_sem,
+):
+    half = block_ref.shape[0] // 2
+    width = mixed_ref.shape[1]
+    extra = block_ref.shape[1] - width
+    expert_count = extra // 2
+    local = gate.shape[0]
+    chunk = 2 * LINE * half
+    slots = LINE * capacity
+    tile = 512
+    tiles = width // tile
+
+    ep, rep = lax.axis_index("ep"), lax.axis_index("rep")
+    z, x, y, core = ep // 2, ep % 2, rep // 2, rep % 2
+    across_x = (z * 2 + (1 - x), rep)
+    across_y = (ep, (1 - y) * 2 + core)
+    sibling = (ep, y * 2 + (1 - core))
+
+    def along_z(step):
+        return (((z + step) % LINE) * 2 + x, rep)
+
+    peers = [across_x, across_y, sibling] + [along_z(step) for step in (1, 2, 3)]
+    barrier = pltpu.get_barrier_semaphore()
+    for peer in peers:
+        pl.semaphore_signal(barrier, inc=1, device_id=peer, device_id_type=MESH)
+    weight_copies = [
+        pltpu.make_async_copy(source, target, weight_sem.at[i])
+        for i, (source, target) in enumerate(((gate_hbm, gate), (up_hbm, up), (down_hbm, down)))
+    ]
+    for copy in weight_copies:
+        copy.start()
+    pl.semaphore_wait(barrier, len(peers))
+
+    started = []
+
+    def send(source, target, device):
+        index = len(started)
+        copy = pltpu.make_async_remote_copy(
+            src_ref=source, dst_ref=target, send_sem=send_sem.at[index],
+            recv_sem=recv_sem.at[index], device_id=device, device_id_type=MESH,
+        )
+        copy.start()
+        started.append(copy)
+        return copy
+
+    rows[0, OWN, 0, 0] = block_ref[:half]
+    rows[0, OWN, 1, 0] = block_ref[half:]
+    order = (0, 1, 3, 2)
+    from_z = {
+        k: send(rows.at[0, OWN, :, 0], rows.at[0, OWN, :, k], along_z(k)) for k in order[1:]
+    }
+    x_low, x_high, y_low, y_high, sib_own = {}, {}, {}, {}, {}
+    for k in order:
+        if k:
+            from_z[k].wait_recv()
+        low, high = rows.at[0, OWN, 0, k], rows.at[0, OWN, 1, k]
+        x_low[k] = send(low, rows.at[0, FLIP_X, 0, k], across_x)
+        y_high[k] = send(high, rows.at[0, FLIP_Y, 1, k], across_y)
+        sib_own[k] = send(rows.at[0, OWN, :, k], rows.at[1, OWN, :, k], sibling)
+        y_low[k] = send(low, rows.at[0, FLIP_Y, 0, k], across_y)
+        x_high[k] = send(high, rows.at[0, FLIP_X, 1, k], across_x)
+    far_low, far_high = {}, {}
+    for k in order:
+        x_low[k].wait_recv()
+        far_low[k] = send(rows.at[0, FLIP_X, 0, k], rows.at[0, FLIP_BOTH, 0, k], across_y)
+        y_high[k].wait_recv()
+        far_high[k] = send(rows.at[0, FLIP_Y, 1, k], rows.at[0, FLIP_BOTH, 1, k], across_x)
+
+    sib_half = {}
+
+    def pass_on(place, part):
+        sib_half[place, part] = send(
+            rows.at[0, place, part], rows.at[1, place, part], sibling
+        )
+
+    pass_on(FLIP_X, 0)
+    pass_on(FLIP_Y, 1)
+
+    column_of = lax.broadcasted_iota(jnp.int32, (16, extra), 1) % expert_count
+    wanted = ep * local + lax.broadcasted_iota(jnp.int32, (16, extra), 0)
+    limit = (ep + 1) * local
+    pick = jnp.where((column_of == wanted) & (wanted < limit), 1.0, 0.0).astype(jnp.bfloat16)
+    above = lax.broadcasted_iota(jnp.int32, (chunk, chunk), 0)
+    below = lax.broadcasted_iota(jnp.int32, (chunk, chunk), 1)
+    earlier = jnp.where(
+        (above < below) & ((above // half) % LINE == (below // half) % LINE), 1.0, 0.0
+    ).astype(jnp.bfloat16)
+    start_slot = (
+        ((lax.broadcasted_iota(jnp.int32, (16, chunk), 1) // half) % LINE) * capacity
+    ).astype(jnp.float32)
+    slot_number = lax.broadcasted_iota(jnp.int32, (slots, chunk), 0).astype(jnp.float32)
+
+    def place_rows(place):
+        for plane in range(2):
+            packed = rows[plane, place, :, :, :, width:].reshape(chunk, extra)
+            weight = lax.dot_general(
+                pick, packed, (((1,), (1,)), ((), ())), preferred_element_type=jnp.float32
+            )
+            mask = jnp.where(weight > 0, 1.0, 0.0)
+            rank = jnp.dot(
+                mask.astype(jnp.bfloat16), earlier, preferred_element_type=jnp.float32
+            )
+            target = jnp.where(mask > 0, start_slot + rank, -1.0)
+            for e in range(local):
+                hit = jnp.where(target[e : e + 1, :] == slot_number, 1.0, 0.0)
+                placing[plane, e] = hit.astype(jnp.bfloat16)
+                total = jnp.sum(hit * weight[e : e + 1, :], axis=1, keepdims=True)
+                slot_weight[e, plane * slots : (plane + 1) * slots, :] = jnp.broadcast_to(
+                    total, (slots, 128)
+                )
+            table = placing[plane].reshape(local * slots, chunk)
+
+            @pl.loop(0, tiles)
+            def _(t):
+                span = pl.ds(pl.multiple_of(t * tile, tile), tile)
+                piece = rows[plane, place, :, :, :, span].reshape(chunk, tile)
+                found = jnp.dot(table, piece, preferred_element_type=jnp.float32)
+                grouped[:, plane * slots : (plane + 1) * slots, span] = found.astype(
+                    jnp.bfloat16
+                ).reshape(local, slots, tile)
+
+    def run_experts():
+        @pl.loop(0, local)
+        def _(e):
+            batch = grouped[e]
+            gate_proj = jnp.dot(batch, gate[e], preferred_element_type=jnp.float32)
+            up_proj = jnp.dot(batch, up[e], preferred_element_type=jnp.float32)
+            active = gate_proj / (1.0 + jnp.exp(-gate_proj)) * up_proj * slot_weight[e][:, :1]
+            active = active.astype(jnp.bfloat16)
+            for t in range(tiles):
+                part = lax.dot_general(
+                    active, down[e, t * tile : (t + 1) * tile, :], (((1,), (1,)), ((), ())),
+                    preferred_element_type=jnp.float32,
+                )
+                grouped[e, :, t * tile : (t + 1) * tile] = part.astype(jnp.bfloat16)
+
+    def combine(plane, place, target, added):
+        table = placing[plane].reshape(local * slots, chunk)
+
+        @pl.loop(0, tiles)
+        def _(t):
+            span = pl.ds(pl.multiple_of(t * tile, tile), tile)
+            piece = grouped[:, plane * slots : (plane + 1) * slots, span]
+            result = lax.dot_general(
+                table, piece.reshape(local * slots, tile), (((0,), (0,)), ((), ())),
+                preferred_element_type=jnp.float32,
+            ).reshape(2, LINE, half, tile)
+            if added is not None:
+                result = result + added[place, :, :, :, span].astype(jnp.float32)
+            target[place, :, :, :, span] = result.astype(jnp.bfloat16)
+
+    def group(place):
+        place_rows(place)
+        run_experts()
+        combine(1, place, sibling_share, None)
+        copy = send(sibling_share.at[place], sibling_sum.at[place], sibling)
+        copy.wait_recv()
+        combine(0, place, share, sibling_sum)
+
+    for k in order:
+        sib_own[k].wait_recv()
+    for copy in weight_copies:
+        copy.wait()
+    group(OWN)
+
+    for k in order:
+        x_high[k].wait_recv()
+        y_low[k].wait_recv()
+    pass_on(FLIP_X, 1)
+    pass_on(FLIP_Y, 0)
+    for k in order:
+        far_low[k].wait_recv()
+        far_high[k].wait_recv()
+    pass_on(FLIP_BOTH, 0)
+    pass_on(FLIP_BOTH, 1)
+
+    for part in range(2):
+        sib_half[FLIP_BOTH, part].wait_recv()
+    group(FLIP_BOTH)
+    y_first = send(share.at[FLIP_BOTH, 0], first_y.at[0], across_y)
+    x_first = send(share.at[FLIP_BOTH, 1], first_x.at[0], across_x)
+    for part in range(2):
+        sib_half[FLIP_X, part].wait_recv()
+    group(FLIP_X)
+    x_next = send(share.at[FLIP_X, 1], first_x.at[1], across_x)
+    for part in range(2):
+        sib_half[FLIP_Y, part].wait_recv()
+    group(FLIP_Y)
+    y_next = send(share.at[FLIP_Y, 0], first_y.at[1], across_y)
+
+    def add_into(target, terms):
+        for k in range(LINE):
+            total = terms[0][k].astype(jnp.float32)
+            for term in terms[1:]:
+                total = total + term[k].astype(jnp.float32)
+            target[k] = total.astype(jnp.bfloat16)
+
+    y_first.wait_recv()
+    low_sum = share.at[FLIP_X, 0]
+    add_into(low_sum, (low_sum, first_y.at[0]))
+    x_last = send(low_sum, second_x, across_x)
+    x_first.wait_recv()
+    high_sum = share.at[FLIP_Y, 1]
+    add_into(high_sum, (high_sum, first_x.at[0]))
+    y_last = send(high_sum, second_y, across_y)
+    x_next.wait_recv()
+    y_next.wait_recv()
+    x_last.wait_recv()
+    add_into(column.at[0], (share.at[OWN, 0], first_y.at[1], second_x))
+    y_last.wait_recv()
+    add_into(column.at[1], (share.at[OWN, 1], first_x.at[1], second_y))
+    ends = [
+        send(column.at[:, k], last.at[k - 1], along_z(LINE - k)) for k in (1, 3, 2)
+    ]
+    for copy in ends:
+        copy.wait_recv()
+    gain = gain_ref[...].astype(jnp.float32)
+    for part in range(2):
+        total = column[part, 0].astype(jnp.float32)
+        for k in range(LINE - 1):
+            total = total + last[k, part].astype(jnp.float32)
+        total = total + mixed_ref[part * half : (part + 1) * half]
+        mean_square = jnp.mean(total * total, axis=-1, keepdims=True)
+        out_ref[part * half : (part + 1) * half] = (
+            total * lax.rsqrt(mean_square + epsilon) * gain
+        ).astype(jnp.bfloat16)
+    for copy in started:
+        copy.wait_send()
+
+
+COPIES = 50
+
+
+def boxed(
+    context, residual, out_proj, attn_gain, router, expert_ids,
+    gate_weight, up_weight, down_weight, final_gain,
+):
+    row_count, width = context.shape
+    mixed_stream, normed, weights = front(
+        context, residual, out_proj, attn_gain, router, expert_ids
+    )
+    top = weights.astype(jnp.bfloat16)
+    rest = (weights - top.astype(jnp.float32)).astype(jnp.bfloat16)
+    block = jnp.concatenate([normed, top, rest], axis=1)
+    half = row_count // 2
+    local = gate_weight.shape[0]
+    slots = LINE * capacity
+    chunk = 2 * LINE * half
+    low = jnp.bfloat16
+    vmem = pl.BlockSpec(memory_space=pltpu.VMEM)
+    hbm = pl.BlockSpec(memory_space=pl.ANY)
+    return pl.pallas_call(
+        box_kernel,
+        out_shape=jax.ShapeDtypeStruct((row_count, width), low),
+        in_specs=[vmem, vmem, vmem, hbm, hbm, hbm],
+        out_specs=vmem,
+        scratch_shapes=[
+            pltpu.VMEM((2, 4, 2, LINE, half, block.shape[1]), low),
+            pltpu.VMEM(gate_weight.shape, low),
+            pltpu.VMEM(up_weight.shape, low),
+            pltpu.VMEM(down_weight.shape, low),
+            pltpu.VMEM((local, 2 * slots, width), low),
+            pltpu.VMEM((2, local, slots, chunk), low),
+            pltpu.VMEM((local, 2 * slots, 128), jnp.float32),
+            pltpu.VMEM((4, 2, LINE, half, width), low),
+            pltpu.VMEM((4, 2, LINE, half, width), low),
+            pltpu.VMEM((4, 2, LINE, half, width), low),
+            pltpu.VMEM((2, LINE, half, width), low),
+            pltpu.VMEM((2, LINE, half, width), low),
+            pltpu.VMEM((LINE, half, width), low),
+            pltpu.VMEM((LINE, half, width), low),
+            pltpu.VMEM((2, LINE, half, width), low),
+            pltpu.VMEM((LINE - 1, 2, half, width), low),
+            pltpu.SemaphoreType.DMA((3,)),
+            pltpu.SemaphoreType.DMA((COPIES,)),
+            pltpu.SemaphoreType.DMA((COPIES,)),
+        ],
+        compiler_params=pltpu.CompilerParams(
+            collective_id=0, has_side_effects=True, vmem_limit_bytes=63 * 1024 * 1024
+        ),
+    )(block, mixed_stream, final_gain.reshape(1, width), gate_weight, up_weight, down_weight)
+
+
 def solution(mesh):
+    per_device = boxed if dict(mesh.shape) == {"ep": 2 * LINE, "rep": 4} else gathered
     in_specs = (
         P(("ep", "rep"), None),
         P(("ep", "rep"), None),
@@ -92,5 +387,5 @@
     )
     out_specs = P(("ep", "rep"), None)
     return jax.shard_map(
-        gathered, mesh=mesh, in_specs=in_specs, out_specs=out_specs, check_vma=False
-    )
+        per_device, mesh=mesh, in_specs=in_specs, out_specs=out_specs, check_vma=False
+    )

time: 330 us -> 166 us (0.50)
  waiting for transfers between devices: 229 us -> 0 us
  Pallas kernels: 0 us -> 156 us
  matrix products: 59.6 us -> 5.39 us
  local copies, waits for them, and re-layouts: 23.3 us -> 4.1 us
  between operations: 13.6 us -> 0.09 us
  other arithmetic: 4.23 us -> 0.58 us
    pallas_call x0 -> x1, Pallas kernels: none -> 156 us  [boxed(): pl.pallas_call(box_kernel, out_shape=jax.ShapeDtypeStruct((row_count, wid...]
    reduce_scatter x1 -> x0, waiting for transfers between devices: 147 us -> none  [gathered(): lax.psum_scatter(share, ('ep', 'rep'), scatter_dimension=0, tiled=True)]
    all_gather x1 -> x0, waiting for transfers between devices: 82.4 us -> none  [gathered(): everyone = lax.all_gather(block, ('ep', 'rep'), axis=0, tiled=False)]
    dot_general x5 -> x0, matrix products: 54.2 us -> none  [the longest x1 20.4 us: gathered(): jnp.einsum('serw,edw->serd', active, down_weight, preferred_element_type=...]
    convert_element_type x1 -> x0, local copies, waits for them, and re-layouts: 14.1 us -> none  [gathered(): part = jnp.einsum('serw,edw->serd', active, down_weight, preferred_elemen...]
    eq x4 -> x0, local copies, waits for them, and re-layouts: 3.77 us -> none  [gathered(): rank[:, :, :, None] == slots]
  transfers between devices with their start and end apart: 2 -> 0, of which waited for: 2 -> 0; matrix products, arithmetic and copies ran while one was open for 0% -> 0% of each run, Pallas kernels for 0% -> 0%
where the time goes in v2:
time: 166 us
  Pallas kernels  156 us (94%)
  matrix products  5.39 us (3%)
  local copies, waits for them, and re-layouts  4.1 us (2%)
    pallas_call x1, Pallas kernels, boxed(): pl.pallas_call(box_kernel, out_shape=jax.ShapeDtypeStruct((row_count, wid...  156 us
    dot_general x1, matrix products, front(): attention = jnp.dot(context, out_proj, preferred_element_type=jnp.float32)  5.07 us

profile of v2, /device:TPU:0, one launch (start us, length us, event | category | flops | bytes accessed | tf_op | source)
XLA Modules:
  0.0 165.8 jit_solution(4081018088022324041)
XLA Ops:
  0.0 0.0 copy-start
  0.0 0.0 copy-start.3
  0.0 0.0 copy-start.2
  0.0 0.0 copy-start.4
  0.0 0.0 copy-start.5
  0.0 0.9 copy-done
  1.0 5.1 %multiply_reduce_fusion = (f32[64]{0:T(128)S(1)}, f32[64,2048]{1,0:T(8,128)S(1)}) fusion(bf16[64,2048]{1,0:T(8,128)(2,1)S(1)} %copy-done, bf16[2048,2048]{1,0:T(8,128)(2,1)} %param.12, bf16[64,2048]{1,0:T(8,128)(2,1)} %param.11), kind=kOutput, calls=%fused_computation.2 | convolution fusion | flops 537395136 | bytes 9437440 | tf_op jit(solution)/shard_map/dot_general | solution.py:19
  6.0 0.0 copy-start.1
  6.1 0.0 copy-done.3
  6.1 0.1 multiply_convert_fusion
  6.2 0.0 copy-done.2
  6.2 0.3 fusion.3
  6.5 0.2 fusion.1
  6.7 0.0 copy-done.4
  6.7 0.1 copy.12
  6.8 0.2 fusion
  7.0 0.1 subtract_convert_fusion
  7.1 0.8 concatenate.3.block_ref
  7.9 0.0 copy-done.5
  7.9 0.6 reshape.15.gain_ref
  8.5 0.0 copy-done.1
  8.5 155.7 %shard_map.100 = bf16[64,2048]{1,0:T(8,128)(2,1)} custom-call(bf16[64,2176]{1,0:T(8,128)(2,1)} %concatenate.3.block_ref, f32[64,2048]{1,0:T(8,128)} %copy-done.1, bf16[1,2048]{1,0:T(2,128)(2,1)} %reshape.15.gain_ref, bf16[8,2048,256]{2,1,0:T(8,128)(2,1)} %gate_hbm.1, bf16[8,2048,256]{2,1,0:T(8,128)(2,1)} %up_hbm.1, bf16[8,2048,256]{2,1,0:T(8,128)(2,1)} %down_hbm.1), custom_call_target="tpu_custom_call" | custom-call | tf_op jit(solution)/shard_map/pallas_call | solution.py:342
  164.2 1.7 %copy.14 = bf16[64,2048]{1,0:T(8,128)(2,1)} copy(bf16[64,2048]{1,0:T(8,128)(2,1)} %shard_map.100) | data formatting | bytes 524288
  (2 shorter events, 0.0 us)
Async XLA Ops:
  0.0 1.0 copy-start
  0.0 6.0 %copy-start.3 = (bf16[2048]{0:T(1024)(128)(2,1)S(1)}, bf16[2048]{0:T(1024)(128)(2,1)}, u32[]{:S(2)}) copy-start(bf16[2048]{0:T(1024)(128)(2,1)} %param.13) | copy-start | bytes 12292
  0.0 6.2 %copy-start.2 = (bf16[2048,64]{0,1:T(8,128)(2,1)S(1)}, bf16[2048,64]{0,1:T(8,128)(2,1)}, u32[]{:S(2)}) copy-start(bf16[2048,64]{0,1:T(8,128)(2,1)} %param.14) | copy-start | bytes 786436
  0.0 6.7 %copy-start.4 = (s32[64,8]{0,1:T(8,128)S(1)}, s32[64,8]{0,1:T(8,128)}, u32[]{:S(2)}) copy-start(s32[64,8]{0,1:T(8,128)} %param.15) | copy-start | bytes 6148
  0.0 7.9 %copy-start.5 = (bf16[2048]{0:T(1024)(128)(2,1)S(1)}, bf16[2048]{0:T(1024)(128)(2,1)}, u32[]{:S(2)}) copy-start(bf16[2048]{0:T(1024)(128)(2,1)} %param.19) | copy-start | bytes 12292
  6.0 2.5 %copy-start.1 = (f32[64,2048]{1,0:T(8,128)}, f32[64,2048]{1,0:T(8,128)S(1)}, u32[]{:S(2)}) copy-start(f32[64,2048]{1,0:T(8,128)S(1)} %get-tuple-element.8.mixed_ref) | copy-start | bytes 1572868

commit v3 on v2

--- a/solution.py
+++ b/solution.py
@@ -150,21 +150,21 @@
         y_low[k] = send(low, rows.at[0, FLIP_Y, 0, k], across_y)
         x_high[k] = send(high, rows.at[0, FLIP_X, 1, k], across_x)
     far_low, far_high = {}, {}
-    for k in order:
+
+    def forward(k):
         x_low[k].wait_recv()
         far_low[k] = send(rows.at[0, FLIP_X, 0, k], rows.at[0, FLIP_BOTH, 0, k], across_y)
         y_high[k].wait_recv()
         far_high[k] = send(rows.at[0, FLIP_Y, 1, k], rows.at[0, FLIP_BOTH, 1, k], across_x)
 
+    for k in order[:2]:
+        forward(k)
     sib_half = {}
 
     def pass_on(place, part):
         sib_half[place, part] = send(
             rows.at[0, place, part], rows.at[1, place, part], sibling
         )
-
-    pass_on(FLIP_X, 0)
-    pass_on(FLIP_Y, 1)
 
     column_of = lax.broadcasted_iota(jnp.int32, (16, extra), 1) % expert_count
     wanted = ep * local + lax.broadcasted_iota(jnp.int32, (16, extra), 0)
@@ -224,10 +224,10 @@
                 )
                 grouped[e, :, t * tile : (t + 1) * tile] = part.astype(jnp.bfloat16)
 
-    def combine(plane, place, target, added):
+    def combine(plane, place, target, added, first_tile):
         table = placing[plane].reshape(local * slots, chunk)
 
-        @pl.loop(0, tiles)
+        @pl.loop(first_tile, first_tile + tiles // 2)
         def _(t):
             span = pl.ds(pl.multiple_of(t * tile, tile), tile)
             piece = grouped[:, plane * slots : (plane + 1) * slots, span]
@@ -239,71 +239,112 @@
                 result = result + added[place, :, :, :, span].astype(jnp.float32)
             target[place, :, :, :, span] = result.astype(jnp.bfloat16)
 
-    def group(place):
+    def group(place, reduced):
         place_rows(place)
         run_experts()
-        combine(1, place, sibling_share, None)
-        copy = send(sibling_share.at[place], sibling_sum.at[place], sibling)
-        copy.wait_recv()
-        combine(0, place, share, sibling_sum)
-
+        copies = []
+        for first_tile in (0, tiles // 2):
+            combine(1, place, sibling_share, None, first_tile)
+            span = pl.ds(first_tile * tile, tiles // 2 * tile)
+            copies.append(
+                send(
+                    sibling_share.at[place, :, :, :, span],
+                    sibling_sum.at[place, :, :, :, span],
+                    sibling,
+                )
+            )
+        for first_tile, copy in zip((0, tiles // 2), copies):
+            if reduced:
+                copy.wait_recv()
+            combine(0, place, share, sibling_sum if reduced else None, first_tile)
+        return copies
+
+    def send_each(source, target, device):
+        return {k: send(source.at[k], target.at[k], device) for k in late}
+
+    late = (2, 1, 3, 0)
     for k in order:
         sib_own[k].wait_recv()
     for copy in weight_copies:
         copy.wait()
-    group(OWN)
-
+    own_copies = group(OWN, False)
+
+    for k in order[2:]:
+        forward(k)
     for k in order:
         x_high[k].wait_recv()
+    pass_on(FLIP_X, 0)
+    pass_on(FLIP_X, 1)
+    for k in order:
         y_low[k].wait_recv()
-    pass_on(FLIP_X, 1)
     pass_on(FLIP_Y, 0)
+    pass_on(FLIP_Y, 1)
+    for part in range(2):
+        sib_half[FLIP_X, part].wait_recv()
+    group(FLIP_X, True)
+    x_next = send_each(share.at[FLIP_X, 1], first_x.at[1], across_x)
     for k in order:
         far_low[k].wait_recv()
         far_high[k].wait_recv()
     pass_on(FLIP_BOTH, 0)
     pass_on(FLIP_BOTH, 1)
-
+    for part in range(2):
+        sib_half[FLIP_Y, part].wait_recv()
+    group(FLIP_Y, True)
+    y_next = send_each(share.at[FLIP_Y, 0], first_y.at[1], across_y)
     for part in range(2):
         sib_half[FLIP_BOTH, part].wait_recv()
-    group(FLIP_BOTH)
-    y_first = send(share.at[FLIP_BOTH, 0], first_y.at[0], across_y)
-    x_first = send(share.at[FLIP_BOTH, 1], first_x.at[0], across_x)
-    for part in range(2):
-        sib_half[FLIP_X, part].wait_recv()
-    group(FLIP_X)
-    x_next = send(share.at[FLIP_X, 1], first_x.at[1], across_x)
-    for part in range(2):
-        sib_half[FLIP_Y, part].wait_recv()
-    group(FLIP_Y)
-    y_next = send(share.at[FLIP_Y, 0], first_y.at[1], across_y)
+    group(FLIP_BOTH, True)
+    y_first, x_first = {}, {}
+    for k in late:
+        y_first[k] = send(share.at[FLIP_BOTH, 0, k], first_y.at[0, k], across_y)
+        x_first[k] = send(share.at[FLIP_BOTH, 1, k], first_x.at[0, k], across_x)
+    for copy in own_copies:
+        copy.wait_recv()
 
     def add_into(target, terms):
-        for k in range(LINE):
-            total = terms[0][k].astype(jnp.float32)
-            for term in terms[1:]:
-                total = total + term[k].astype(jnp.float32)
-            target[k] = total.astype(jnp.bfloat16)
-
-    y_first.wait_recv()
-    low_sum = share.at[FLIP_X, 0]
-    add_into(low_sum, (low_sum, first_y.at[0]))
-    x_last = send(low_sum, second_x, across_x)
-    x_first.wait_recv()
-    high_sum = share.at[FLIP_Y, 1]
-    add_into(high_sum, (high_sum, first_x.at[0]))
-    y_last = send(high_sum, second_y, across_y)
-    x_next.wait_recv()
-    y_next.wait_recv()
-    x_last.wait_recv()
-    add_into(column.at[0], (share.at[OWN, 0], first_y.at[1], second_x))
-    y_last.wait_recv()
-    add_into(column.at[1], (share.at[OWN, 1], first_x.at[1], second_y))
-    ends = [
-        send(column.at[:, k], last.at[k - 1], along_z(LINE - k)) for k in (1, 3, 2)
-    ]
-    for copy in ends:
+        total = terms[0][...].astype(jnp.float32)
+        for term in terms[1:]:
+            total = total + term[...].astype(jnp.float32)
+        target[...] = total.astype(jnp.bfloat16)
+
+    x_last, y_last, ends = {}, {}, {}
+
+    def turn(k):
+        y_first[k].wait_recv()
+        low_sum = share.at[FLIP_X, 0, k]
+        add_into(low_sum, (low_sum, first_y.at[0, k]))
+        x_last[k] = send(low_sum, second_x.at[k], across_x)
+        x_first[k].wait_recv()
+        high_sum = share.at[FLIP_Y, 1, k]
+        add_into(high_sum, (high_sum, first_x.at[0, k]))
+        y_last[k] = send(high_sum, second_y.at[k], across_y)
+
+    def finish(k):
+        y_next[k].wait_recv()
+        x_last[k].wait_recv()
+        add_into(
+            column.at[0, k],
+            (share.at[OWN, 0, k], sibling_sum.at[OWN, 0, k], first_y.at[1, k], second_x.at[k]),
+        )
+        x_next[k].wait_recv()
+        y_last[k].wait_recv()
+        add_into(
+            column.at[1, k],
+            (share.at[OWN, 1, k], sibling_sum.at[OWN, 1, k], first_x.at[1, k], second_y.at[k]),
+        )
+        if k:
+            ends[k] = send(column.at[:, k], last.at[k - 1], along_z(LINE - k))
+
+    turn(late[0])
+    turn(late[1])
+    for i, k in enumerate(late):
+        finish(k)
+        if i + 2 < LINE:
+            turn(late[i + 2])
+    for copy in ends.values():
         copy.wait_recv()
+    assert len(started) == COPIES, len(started)
     gain = gain_ref[...].astype(jnp.float32)
     for part in range(2):
         total = column[part, 0].astype(jnp.float32)
@@ -318,7 +359,7 @@
         copy.wait_send()
 
 
-COPIES = 50
+COPIES = 72
 
 
 def boxed(

time: 166 us -> 138 us (0.83)
  Pallas kernels: 156 us -> 127 us
    pallas_call x1, Pallas kernels: 156 us -> 127 us  [boxed(): pl.pallas_call(box_kernel, out_shape=jax.ShapeDtypeStruct((row_count, wid...]
where the time goes in v3:
time: 138 us; the launch traced here: 137 us
  Pallas kernels  127 us (92%)
  matrix products  5.39 us (4%)
  local copies, waits for them, and re-layouts  4.1 us (3%)
    pallas_call x1, Pallas kernels, boxed(): pl.pallas_call(box_kernel, out_shape=jax.ShapeDtypeStruct((row_count, wid...  127 us
    dot_general x1, matrix products, front(): attention = jnp.dot(context, out_proj, preferred_element_type=jnp.float32)  5.07 us

profile of v3, /device:TPU:0, one launch (start us, length us, event | category | flops | bytes accessed | tf_op | source)
XLA Modules:
  0.0 137.2 jit_solution(3107047010182026906)
XLA Ops:
  0.0 0.0 copy-start
  0.0 0.0 copy-start.3
  0.0 0.0 copy-start.2
  0.0 0.0 copy-start.4
  0.0 0.0 copy-start.5
  0.0 0.9 copy-done
  1.0 5.1 %multiply_reduce_fusion = (f32[64]{0:T(128)S(1)}, f32[64,2048]{1,0:T(8,128)S(1)}) fusion(bf16[64,2048]{1,0:T(8,128)(2,1)S(1)} %copy-done, bf16[2048,2048]{1,0:T(8,128)(2,1)} %param.12, bf16[64,2048]{1,0:T(8,128)(2,1)} %param.11), kind=kOutput, calls=%fused_computation.2 | convolution fusion | flops 537395136 | bytes 9437440 | tf_op jit(solution)/shard_map/dot_general | solution.py:19
  6.0 0.0 copy-start.1
  6.1 0.0 copy-done.3
  6.1 0.1 multiply_convert_fusion
  6.2 0.0 copy-done.2
  6.2 0.3 fusion.3
  6.5 0.2 fusion.1
  6.7 0.0 copy-done.4
  6.7 0.1 copy.12
  6.8 0.2 fusion
  7.0 0.1 subtract_convert_fusion
  7.1 0.8 concatenate.3.block_ref
  7.9 0.0 copy-done.5
  7.9 0.6 reshape.15.gain_ref
  8.5 0.0 copy-done.1
  8.5 127.1 %shard_map.100 = bf16[64,2048]{1,0:T(8,128)(2,1)} custom-call(bf16[64,2176]{1,0:T(8,128)(2,1)} %concatenate.3.block_ref, f32[64,2048]{1,0:T(8,128)} %copy-done.1, bf16[1,2048]{1,0:T(2,128)(2,1)} %reshape.15.gain_ref, bf16[8,2048,256]{2,1,0:T(8,128)(2,1)} %gate_hbm.1, bf16[8,2048,256]{2,1,0:T(8,128)(2,1)} %up_hbm.1, bf16[8,2048,256]{2,1,0:T(8,128)(2,1)} %down_hbm.1), custom_call_target="tpu_custom_call" | custom-call | tf_op jit(solution)/shard_map/pallas_call | solution.py:383
  135.6 1.7 %copy.14 = bf16[64,2048]{1,0:T(8,128)(2,1)} copy(bf16[64,2048]{1,0:T(8,128)(2,1)} %shard_map.100) | data formatting | bytes 524288
  (2 shorter events, 0.0 us)
Async XLA Ops:
  0.0 1.0 copy-start
  0.0 6.0 %copy-start.3 = (bf16[2048]{0:T(1024)(128)(2,1)S(1)}, bf16[2048]{0:T(1024)(128)(2,1)}, u32[]{:S(2)}) copy-start(bf16[2048]{0:T(1024)(128)(2,1)} %param.13) | copy-start | bytes 12292
  0.0 6.2 %copy-start.2 = (bf16[2048,64]{0,1:T(8,128)(2,1)S(1)}, bf16[2048,64]{0,1:T(8,128)(2,1)}, u32[]{:S(2)}) copy-start(bf16[2048,64]{0,1:T(8,128)(2,1)} %param.14) | copy-start | bytes 786436
  0.0 6.7 %copy-start.4 = (s32[64,8]{0,1:T(8,128)S(1)}, s32[64,8]{0,1:T(8,128)}, u32[]{:S(2)}) copy-start(s32[64,8]{0,1:T(8,128)} %param.15) | copy-start | bytes 6148
  0.0 7.9 %copy-start.5 = (bf16[2048]{0:T(1024)(128)(2,1)S(1)}, bf16[2048]{0:T(1024)(128)(2,1)}, u32[]{:S(2)}) copy-start(bf16[2048]{0:T(1024)(128)(2,1)} %param.19) | copy-start | bytes 12292
  6.0 2.5 %copy-start.1 = (f32[64,2048]{1,0:T(8,128)}, f32[64,2048]{1,0:T(8,128)S(1)}, u32[]{:S(2)}) copy-start(f32[64,2048]{1,0:T(8,128)S(1)} %get-tuple-element.8.mixed_ref) | copy-start | bytes 1572868
